TPU v7x, 512 devices: a whole 4x4x16 slice. The times are simulated.
512 devices in a mesh: blk: 8 (over y_lo, x), rows: 64 (over z, y_hi, core).
Axes of the slice: x: 4, y: 4 (y_hi: 2, y_lo: 2; y = y_hi * 2 + y_lo), z: 16, core: 2. Of those that a mesh axis runs over, the one named last changes fastest.
Arguments:
- queries: bfloat16 [128, 4, 8192], P('rows', None, 'blk'), may hold values from -36 to 36
- new_entries: bfloat16 [128, 4, 2, 1024], P('rows', None, None, 'blk'), may hold values from -9 to 9
- resident: bfloat16 [4096, 2, 16, 1024], P('rows', None, None, 'blk'), may hold values from -9 to 9
- swap_area: bfloat16 [4096, 2, 16, 1024], P('rows', None, None, 'blk'), may hold values from -9 to 9
- swap_dest: int32 [4096], P('rows'), may hold values from 0 to 63, as said below
- page_table: int32 [128, 64], P('rows'), may hold values from 0 to 191, as said below
- lengths: int32 [128], P('rows'), may hold values from 256 to 1024, as said below
- norm_gain: bfloat16 [8192], P('blk'), may hold values from 0.099609375 to 1.8984375
- gate_weight: bfloat16 [8192, 28672], P('blk', 'rows'), may hold values from -0.0625 to 0.0625
- up_weight: bfloat16 [8192, 28672], P('blk', 'rows'), may hold values from -0.0625 to 0.0625
- down_weight: bfloat16 [28672, 8192], P('rows', 'blk'), may hold values from -0.03125 to 0.03125
Outputs:
- attended: bfloat16 [128, 4, 8192], P('rows', None, 'blk')
- layer_out: bfloat16 [128, 4, 8192], P('rows', None, 'blk')
Inputs may be any that keep to these rules, and one draw needn't show every extreme that they name: `swap_dest`: every owner sends exactly 2 of its pages to each of 32 different owners (possibly itself), and every owner receives exactly 64 pages. `page_table`: the entries of the 2 rows of one owner name each of its 64 resident pages and each of the 64 pages that land there exactly once; an entry at or above 64 is 64 + s * 2 + k for the k-th page, in the order of the sender's pages, that owner s sends to the row's owner. `lengths`: some row has exactly 1024 cached positions.
All inputs are finite; a program needn't handle non-finite values.
Results may differ from a plain program's by a relative error of at most 0.0086.
Values may be sent and summed in bfloat16 or wider, within the bound.
No kernel may reach another device: no remote copies, remote signals or barrier semaphores. Data moves between devices by JAX's collectives and lax.ppermute only.
A program may use at most 64 MiB of HBM per device.

v0:
```python
import math
import jax
import jax.numpy as jnp
from jax import lax
from jax.sharding import PartitionSpec as P

GQ = 8
HD = 128
PAGE = 16
CAP = 2
epsilon = 1e-05


def on_device(
    queries,
    new_entries,
    resident,
    swap_area,
    swap_dest,
    page_table,
    lengths,
    norm_gain,
    gate_weight,
    up_weight,
    down_weight,
):
    owners = lax.axis_size("rows")
    swap_count = swap_area.shape[0]
    page_width = swap_area.shape[1] * swap_area.shape[2] * swap_area.shape[3]
    flat_swap = swap_area.reshape(swap_count, page_width)
    target = swap_dest[:, None] == jnp.arange(owners, dtype=jnp.int32)[None, :]
    before = jnp.cumsum(target.astype(jnp.int32), axis=0) - 1
    page_rank = jnp.sum(jnp.where(target, before, 0), axis=1)
    send_slot = swap_dest * CAP + page_rank
    placement = (jnp.arange(owners * CAP, dtype=jnp.int32)[:, None] == send_slot[None, :]).astype(
        jnp.bfloat16
    )
    outgoing = jnp.dot(placement, flat_swap, preferred_element_type=jnp.float32).astype(
        jnp.bfloat16
    )
    outgoing = outgoing.reshape(owners, CAP, page_width)
    arrived = lax.all_to_all(outgoing, "rows", split_axis=0, concat_axis=0, tiled=True)
    page_store = jnp.concatenate(
        [resident.reshape(-1, page_width), arrived.reshape(owners * CAP, page_width)], axis=0
    )
    fetched = page_store[page_table]
    rows_here, pages_row = page_table.shape
    step_count = queries.shape[1]
    kv_heads = new_entries.shape[-1] // HD
    fetched = fetched.reshape(rows_here, pages_row, 2, PAGE, kv_heads, HD)
    cached_keys = fetched[:, :, 0].reshape(rows_here, pages_row * PAGE, kv_heads, HD)
    cached_values = fetched[:, :, 1].reshape(rows_here, pages_row * PAGE, kv_heads, HD)
    head_queries = queries.reshape(rows_here, step_count, kv_heads, GQ, HD)
    step_entries = new_entries.reshape(rows_here, step_count, 2, kv_heads, HD)
    score_scale = 1.0 / math.sqrt(HD)
    cached_scores = (
        jnp.einsum(
            "rskgd,rlkd->rkgsl", head_queries, cached_keys, preferred_element_type=jnp.float32
        )
        * score_scale
    )
    new_scores = (
        jnp.einsum(
            "rskgd,rtkd->rkgst",
            head_queries,
            step_entries[:, :, 0],
            preferred_element_type=jnp.float32,
        )
        * score_scale
    )
    visible = jnp.arange(pages_row * PAGE, dtype=jnp.int32)[None, :] < lengths[:, None]
    causal = jnp.arange(step_count)[None, :] <= jnp.arange(step_count)[:, None]
    cached_scores = jnp.where(visible[:, None, None, None, :], cached_scores, -1e30)
    new_scores = jnp.where(causal[None, None, None], new_scores, -1e30)
    row_peak = jnp.maximum(jnp.max(cached_scores, axis=-1), jnp.max(new_scores, axis=-1))[..., None]
    cached_exp = jnp.exp(cached_scores - row_peak)
    new_exp = jnp.exp(new_scores - row_peak)
    row_total = (jnp.sum(cached_exp, axis=-1) + jnp.sum(new_exp, axis=-1))[..., None]
    cached_weights = (cached_exp / row_total).astype(jnp.bfloat16)
    new_weights = (new_exp / row_total).astype(jnp.bfloat16)
    mixed_heads = jnp.einsum(
        "rkgsl,rlkd->rskgd", cached_weights, cached_values, preferred_element_type=jnp.float32
    )
    mixed_heads = mixed_heads + jnp.einsum(
        "rkgst,rtkd->rskgd", new_weights, step_entries[:, :, 1], preferred_element_type=jnp.float32
    )
    attended = mixed_heads.reshape(rows_here, step_count, -1).astype(jnp.bfloat16)
    local_tokens = attended.reshape(rows_here * step_count, -1)
    gathered = lax.all_gather(local_tokens, "rows", axis=0, tiled=True)
    gathered_wide = gathered.astype(jnp.float32)
    squares = jnp.sum(gathered_wide * gathered_wide, axis=1)
    normed = (gathered_wide * norm_gain.astype(jnp.float32)[None, :]).astype(jnp.bfloat16)
    gate_part = jnp.dot(normed, gate_weight, preferred_element_type=jnp.float32)
    up_part = jnp.dot(normed, up_weight, preferred_element_type=jnp.float32)
    width_total = gathered.shape[1] * lax.axis_size("blk")
    gate_sum, up_sum, square_sum = lax.psum((gate_part, up_part, squares), "blk")
    factor = lax.rsqrt(square_sum / width_total + epsilon)[:, None]
    hidden = (jax.nn.silu(factor * gate_sum) * (factor * up_sum)).astype(jnp.bfloat16)
    down_sum = lax.psum_scatter(
        jnp.dot(hidden, down_weight, preferred_element_type=jnp.float32),
        "rows",
        scatter_dimension=0,
        tiled=True,
    )
    layer_out = (local_tokens.astype(jnp.float32) + down_sum).astype(jnp.bfloat16)
    return (attended, layer_out.reshape(rows_here, step_count, -1))


def solution(mesh):
    placed = (
        P("rows", None, "blk"),
        P("rows", None, None, "blk"),
        P("rows", None, None, "blk"),
        P("rows", None, None, "blk"),
        P("rows"),
        P("rows", None),
        P("rows"),
        P("blk"),
        P("blk", "rows"),
        P("blk", "rows"),
        P("rows", "blk"),
    )
    return jax.shard_map(
        on_device,
        mesh=mesh,
        in_specs=placed,
        out_specs=(P("rows", None, "blk"), P("rows", None, "blk")),
        check_vma=False,
    )
```

profile of v0, /device:TPU:2, one launch (start us, length us, event | category | flops | bytes accessed | tf_op | source)
XLA Modules:
  0.0 548.7 jit_solution(16742943073197080970)
XLA Ops:
  7.2 0.0 copy-start
  7.2 0.8 fusion.23
  8.0 0.1 reduce_window_sum.11
  8.1 0.8 select_reduce_fusion
  8.9 0.7 multiply_add_fusion
  9.6 1.5 convolution_convert_fusion
  11.1 0.0 copy-start.11
  11.1 0.0 copy-start.7
  11.1 0.0 copy-start.5
  11.1 0.0 copy-start.2
  11.1 1.5 reshape.143
  12.6 18.9 %all-to-all-start = ((bf16[64,2,4096]{2,1,0:T(2,128)(2,1)}), bf16[64,2,4096]{2,1,0:T(2,128)(2,1)S(1)}, u32[]{:S(2)}, u32[]{:S(2)}) async-start(bf16[64,2,4096]{2,1,0:T(2,128)(2,1)} %reshape.143), calls=%async_computation | async-start | bytes 2097152 | tf_op jit(solution)/shard_map/all_to_all | solution.py:42
  31.5 0.0 all-gather.2.cloned.1.call-start
  31.6 0.0 copy-done.11
  31.6 0.1 reshape.157
  31.7 0.0 copy-done.7
  31.7 0.0 copy-done.5
  31.7 0.0 copy-start.8
  31.7 0.0 copy-done.2
  31.7 1.0 copy.35
  32.7 0.6 pad_clamp_fusion
  33.3 0.0 copy-done.12
  33.3 0.7 iota_compare_fusion.3
  34.0 1.4 fusion.30
  35.4 0.0 copy-done.8
  35.4 52.2 %all-to-all-done = bf16[64,2,4096]{2,1,0:T(2,128)(2,1)S(1)} async-done(((bf16[64,2,4096]{2,1,0:T(2,128)(2,1)}), bf16[64,2,4096]{2,1,0:T(2,128)(2,1)S(1)}, u32[]{:S(2)}, u32[]{:S(2)}) %all-to-all-start) | async-done | bytes 1048608 | tf_op jit(solution)/shard_map/all_to_all | solution.py:42
  87.6 0.4 reshape.144
  88.1 1.2 pad_maximum_fusion
  89.3 1.3 gather_fusion
  90.6 0.0 copy-start.3
  90.6 0.0 copy-start.6
  90.6 0.0 copy-start.4
  90.6 0.2 copy.24
  90.9 0.0 copy-start.9
  90.9 0.0 copy-start.10
  90.9 0.0 copy-start.13
  90.9 0.2 fusion.28
  91.1 0.2 copy-done.3
  91.3 0.4 fusion.29
  91.6 0.0 copy-done.6
  91.6 0.0 copy-done.4
  91.7 0.2 fusion.18
  91.9 0.3 fusion.19
  92.2 0.0 copy-done.9
  92.2 0.2 fusion.6
  92.4 0.6 copy.36
  93.0 0.0 all-gather.2.cloned.1.call-update
  93.0 0.0 all-reduce.3.cloned.1.call-start
  93.1 0.0 copy-done.10
  93.1 130.8 %all-gather.2.cloned.1.call-done = bf16[512,1024]{1,0:T(8,128)(2,1)} async-done(((bf16[8,1024]{1,0:T(8,128)(2,1)}), bf16[512,1024]{1,0:T(8,128)(2,1)}) %all-gather.2.cloned.1.call-update) | async-done | bytes 1048592 | tf_op jit(solution)/shard_map/all_gather | solution.py:89
  223.9 0.0 copy-done.13
  223.9 3.0 fusion.9
  226.9 2.8 fusion.11
  229.7 0.0 all-reduce.3.cloned.1.call-update
  229.7 0.0 reduce-scatter.2.cloned.1.call-start
  229.7 0.3 fusion
  230.0 16.5 %psum.21 = f32[512]{0:T(512)S(1)} all-reduce(f32[512]{0:T(512)S(1)} %fusion), channel_id=1, replica_groups=mesh['blk'=8,'rows'=64] {'blk'}, use_global_device_ids=true, to_apply=%region_7.8 | all-reduce | flops 512 | bytes 4096 | tf_op jit(solution)/shard_map/psum | solution.py:96
  246.5 74.4 %all-reduce.3.cloned.1.call-done = (f32[512,448]{0,1:T(8,128)}, f32[512,448]{0,1:T(8,128)}) async-done(((f32[512,448]{0,1:T(8,128)}, f32[512,448]{0,1:T(8,128)}), (f32[512,448]{0,1:T(8,128)}, f32[512,448]{0,1:T(8,128)})) %all-reduce.3.cloned.1.call-update) | async-done | bytes 1835024 | tf_op jit(solution)/shard_map/psum | solution.py:96
  321.0 3.6 fusion.15
  324.6 0.0 reduce-scatter.2.cloned.1.call-update
  324.6 0.6 convert_element_type.56
  325.2 215.6 %reduce-scatter.2.cloned.1.call-done = f32[8,1024]{1,0:T(8,128)} async-done(((f32[512,1024]{1,0:T(8,128)}), f32[8,1024]{1,0:T(8,128)}) %reduce-scatter.2.cloned.1.call-update) | async-done | bytes 32784 | tf_op jit(solution)/shard_map/reduce_scatter | solution.py:99
  540.8 0.8 add_convert_fusion
  541.6 0.6 reshape.154
  (13 shorter events, 0.1 us)
Async XLA Ops:
  7.2 313.8 %copy-start = (bf16[448,1024]{1,0:T(8,128)(2,1)S(1)}, bf16[448,1024]{1,0:T(8,128)(2,1)}, u32[]{:S(2)}) copy-start(bf16[448,1024]{1,0:T(8,128)(2,1)} %param.21) | copy-start | bytes 2752516
  11.1 20.5 %copy-start.11 = (s32[2,64]{1,0:T(2,128)S(1)}, s32[2,64]{1,0:T(2,128)}, u32[]{:S(2)}) copy-start(s32[2,64]{1,0:T(2,128)} %param.16) | copy-start | bytes 1540
  11.1 20.6 %copy-start.7 = (bf16[2,4,2,128]{3,2,1,0:T(2,128)(2,1)S(1)}, bf16[2,4,2,128]{3,2,1,0:T(2,128)(2,1)}, u32[]{:S(2)}) copy-start(bf16[2,4,2,128]{3,2,1,0:T(2,128)(2,1)} %param.12) | copy-start | bytes 12292
  11.1 20.6 %copy-start.5 = (bf16[2,4,1024]{2,1,0:T(4,128)(2,1)S(1)}, bf16[2,4,1024]{2,1,0:T(4,128)(2,1)}, u32[]{:S(2)}) copy-start(bf16[2,4,1024]{2,1,0:T(4,128)(2,1)} %param.11) | copy-start | bytes 49156
  11.1 20.6 %copy-start.2 = (bf16[64,2,16,128]{3,2,1,0:T(8,128)(2,1)S(1)}, bf16[64,2,16,128]{3,2,1,0:T(8,128)(2,1)}, u32[]{:S(2)}) copy-start(bf16[64,2,16,128]{3,2,1,0:T(8,128)(2,1)} %param.13) | copy-start | bytes 1572868
  12.6 20.7 %copy-start.12 = (s32[2]{0:T(128)S(1)}, s32[2]{0:T(128)}, u32[]{:S(2)}) copy-start(s32[2]{0:T(128)} %param.17) | copy-start | bytes 28
  12.6 75.0 %all-to-all-start = ((bf16[64,2,4096]{2,1,0:T(2,128)(2,1)}), bf16[64,2,4096]{2,1,0:T(2,128)(2,1)S(1)}, u32[]{:S(2)}, u32[]{:S(2)}) async-start(bf16[64,2,4096]{2,1,0:T(2,128)(2,1)} %reshape.143), calls=%async_computation | async-start | bytes 2097152 | tf_op jit(solution)/shard_map/all_to_all | solution.py:42
  31.5 192.4 %all-gather.2.cloned.1.call-start = ((), (), s32[]{:S(2)}) async-start(), calls=%async_computation.2 | async-start | bytes 1064960 | tf_op jit(solution)/shard_map/all_gather | solution.py:89
  31.7 3.7 copy-start.8
  90.6 0.7 copy-start.3
  90.6 1.0 copy-start.6
  90.6 1.0 copy-start.4
  90.9 1.3 copy-start.9
  90.9 2.2 copy-start.10
  90.9 133.0 %copy-start.13 = (bf16[1024,448]{0,1:T(8,128)(2,1)S(1)}, bf16[1024,448]{0,1:T(8,128)(2,1)}, u32[]{:S(2)}) copy-start(bf16[1024,448]{0,1:T(8,128)(2,1)} %param.20) | copy-start | bytes 2752516
  93.0 228.0 %all-reduce.3.cloned.1.call-start = ((), (), s32[]{:S(2)}) async-start(), calls=%async_computation.4 | async-start | bytes 3670016 | tf_op jit(solution)/shard_map/psum | solution.py:96
  223.9 3.0 copy-start.1
  229.7 311.1 %reduce-scatter.2.cloned.1.call-start = ((), (), s32[]{:S(2)}) async-start(), calls=%async_computation.3 | async-start | bytes 2129920 | tf_op jit(solution)/shard_map/reduce_scatter | solution.py:99
Sparse Core Ops, SparseCore 0:
  93.1 130.7 all-gather.1
  229.8 91.1 all-reduce.2
  325.6 215.1 reduce-scatter.1
where the time goes:
time: 549 us
  waiting for transfers between devices  473 us (86%)
  starting transfers between devices  19 us (3%)
  blocking collectives  16.5 us (3%)
  between operations  14 us (3%)
  matrix products  13.1 us (2%)
  local copies, waits for them, and re-layouts  6.88 us (1%)
  other arithmetic  6.15 us (1%)
    reduce_scatter x1, waiting for transfers between devices, on_device(): lax.psum_scatter(jnp.dot(hidden, down_weight, preferred_element_type=jnp....  216 us
    all_gather x1, waiting for transfers between devices, on_device(): gathered = lax.all_gather(local_tokens, 'rows', axis=0, tiled=True)  131 us
    psum x1, waiting for transfers between devices, on_device(): lax.psum((gate_part, up_part, squares), 'blk')  74.4 us
    all_to_all x1, waiting for transfers between devices, on_device(): lax.all_to_all(outgoing, 'rows', split_axis=0, concat_axis=0, tiled=True)  52.2 us
    all_to_all x1, starting transfers between devices, on_device(): lax.all_to_all(outgoing, 'rows', split_axis=0, concat_axis=0, tiled=True)  18.9 us
    psum x1, blocking collectives, on_device(): lax.psum((gate_part, up_part, squares), 'blk')  16.5 us
  transfers between devices with their start and end apart: 4, of which 4 were waited for; matrix products, arithmetic and copies ran while one was open for 1% of the time, Pallas kernels for 0%

commit v1 on v0

--- a/solution.py
+++ b/solution.py
@@ -86,7 +86,8 @@
     )
     attended = mixed_heads.reshape(rows_here, step_count, -1).astype(jnp.bfloat16)
     local_tokens = attended.reshape(rows_here * step_count, -1)
-    gathered = lax.all_gather(local_tokens, "rows", axis=0, tiled=True)
+    stack = jnp.stack([local_tokens] * lax.axis_size("rows"))
+    gathered = jnp.concatenate(lax.all_to_all(stack, "rows", 0, 0), axis=0)
     gathered_wide = gathered.astype(jnp.float32)
     squares = jnp.sum(gathered_wide * gathered_wide, axis=1)
     normed = (gathered_wide * norm_gain.astype(jnp.float32)[None, :]).astype(jnp.bfloat16)

time: 549 us -> 474 us (0.86)
  the two profiles are of different devices: /device:TPU:2 before, /device:TPU:4 now
where the time goes in v1:
time: 474 us; the launch traced here: 473 us
  waiting for transfers between devices  394 us (83%)
  starting transfers between devices  24.2 us (5%)
  blocking collectives  15.8 us (3%)
  between operations  14.3 us (3%)
  matrix products  10.6 us (2%)
  local copies, waits for them, and re-layouts  7.53 us (2%)
  other arithmetic  6.16 us (1%)
    reduce_scatter x1, waiting for transfers between devices, on_device(): lax.psum_scatter(jnp.dot(hidden, down_weight, preferred_element_type=jnp....  216 us
    psum x1, waiting for transfers between devices, on_device(): lax.psum((gate_part, up_part, squares), 'blk')  69.8 us
    all_to_all x1, waiting for transfers between devices, on_device(): gathered = jnp.concatenate(lax.all_to_all(stack, 'rows', 0, 0), axis=0)  56.1 us
    all_to_all x1, waiting for transfers between devices, on_device(): lax.all_to_all(outgoing, 'rows', split_axis=0, concat_axis=0, tiled=True)  52.3 us
    all_to_all x1, starting transfers between devices, on_device(): lax.all_to_all(outgoing, 'rows', split_axis=0, concat_axis=0, tiled=True)  18.9 us
    psum x1, blocking collectives, on_device(): lax.psum((gate_part, up_part, squares), 'blk')  15.8 us
  transfers between devices with their start and end apart: 4, of which 4 were waited for; matrix products, arithmetic and copies ran while one was open for 1% of the time, Pallas kernels for 0%

profile of v1, /device:TPU:4, one launch (start us, length us, event | category | flops | bytes accessed | tf_op | source)
XLA Modules:
  0.0 473.0 jit_solution(3177475162041783183)
XLA Ops:
  7.2 0.0 copy-start
  7.2 0.8 fusion.24
  8.0 0.1 reduce_window_sum.11
  8.1 0.8 select_reduce_fusion
  8.9 0.7 multiply_add_fusion
  9.6 1.5 convolution_convert_fusion
  11.1 0.0 copy-start.10
  11.1 0.0 copy-start.6
  11.1 0.0 copy-start.4
  11.1 0.0 copy-start.1
  11.1 1.5 reshape.150
  12.6 18.9 %all-to-all-start = ((bf16[64,2,4096]{2,1,0:T(2,128)(2,1)}), bf16[64,2,4096]{2,1,0:T(2,128)(2,1)S(1)}, u32[]{:S(2)}, u32[]{:S(2)}) async-start(bf16[64,2,4096]{2,1,0:T(2,128)(2,1)} %reshape.150), calls=%async_computation | async-start | bytes 2097152 | tf_op jit(solution)/shard_map/all_to_all | solution.py:42
  31.5 0.0 copy-done.10
  31.5 0.1 reshape.165
  31.6 0.0 copy-done.6
  31.6 0.0 copy-done.4
  31.6 0.0 copy-start.7
  31.6 0.0 copy-done.1
  31.7 1.0 copy.41
  32.7 0.6 pad_clamp_fusion
  33.3 0.0 copy-done.11
  33.3 0.7 iota_compare_fusion.3
  34.0 1.4 fusion.31
  35.3 0.0 copy-done.7
  35.3 52.3 %all-to-all-done = bf16[64,2,4096]{2,1,0:T(2,128)(2,1)S(1)} async-done(((bf16[64,2,4096]{2,1,0:T(2,128)(2,1)}), bf16[64,2,4096]{2,1,0:T(2,128)(2,1)S(1)}, u32[]{:S(2)}, u32[]{:S(2)}) %all-to-all-start) | async-done | bytes 1048608 | tf_op jit(solution)/shard_map/all_to_all | solution.py:42
  87.6 0.4 reshape.151
  88.1 1.2 pad_maximum_fusion
  89.3 1.3 gather_fusion
  90.6 0.0 copy-start.2
  90.6 0.0 copy-start.5
  90.6 0.0 copy-start.3
  90.6 0.2 copy.30
  90.9 0.0 copy-start.8
  90.9 0.2 fusion.29
  91.1 0.2 copy-done.2
  91.3 0.4 fusion.30
  91.6 0.0 copy-done.5
  91.6 0.0 copy-done.3
  91.7 0.2 fusion.19
  91.9 0.0 copy-start.12
  91.9 0.3 fusion.20
  92.2 0.0 copy-done.8
  92.2 0.2 fusion.7
  92.4 1.1 stack.3
  93.5 5.3 %all-to-all-start.1 = ((bf16[64,8,1024]{2,1,0:T(8,128)(2,1)}), bf16[64,8,1024]{2,1,0:T(8,128)(2,1)S(1)}, u32[]{:S(2)}, u32[]{:S(2)}) async-start(bf16[64,8,1024]{2,1,0:T(8,128)(2,1)} %stack.3), calls=%async_computation.1 | async-start | bytes 2097152 | tf_op jit(solution)/shard_map/all_to_all | solution.py:90
  98.8 0.0 all-reduce.3.cloned.1.call-start
  98.9 0.0 copy-done.9
  98.9 56.1 %all-to-all-done.1 = bf16[64,8,1024]{2,1,0:T(8,128)(2,1)S(1)} async-done(((bf16[64,8,1024]{2,1,0:T(8,128)(2,1)}), bf16[64,8,1024]{2,1,0:T(8,128)(2,1)S(1)}, u32[]{:S(2)}, u32[]{:S(2)}) %all-to-all-start.1) | async-done | bytes 1048608 | tf_op jit(solution)/shard_map/all_to_all | solution.py:90
  155.0 0.0 copy-done.12
  155.0 1.6 fusion.10
  156.6 0.0 copy-done.13
  156.6 1.7 fusion.12
  158.2 0.0 all-reduce.3.cloned.1.call-update
  158.3 0.0 reduce-scatter.2.cloned.1.call-start
  158.3 0.3 fusion
  158.6 0.1 reduce_sum.42
  158.7 15.8 %psum.21 = f32[512]{0:T(512)S(1)} all-reduce(f32[512]{0:T(512)S(1)} %reduce_sum.42), channel_id=1, replica_groups=mesh['blk'=8,'rows'=64] {'blk'}, use_global_device_ids=true, to_apply=%region_7.8 | all-reduce | flops 512 | bytes 4096 | tf_op jit(solution)/shard_map/psum | solution.py:97
  174.5 69.8 %all-reduce.3.cloned.1.call-done = (f32[512,448]{0,1:T(8,128)}, f32[512,448]{0,1:T(8,128)}) async-done(((f32[512,448]{0,1:T(8,128)}, f32[512,448]{0,1:T(8,128)}), (f32[512,448]{0,1:T(8,128)}, f32[512,448]{0,1:T(8,128)})) %all-reduce.3.cloned.1.call-update) | async-done | bytes 1835024 | tf_op jit(solution)/shard_map/psum | solution.py:97
  244.2 3.6 fusion.16
  247.8 0.0 reduce-scatter.2.cloned.1.call-update
  247.9 0.6 convert_element_type.64
  248.5 216.4 %reduce-scatter.2.cloned.1.call-done = f32[8,1024]{1,0:T(8,128)} async-done(((f32[512,1024]{1,0:T(8,128)}), f32[8,1024]{1,0:T(8,128)}) %reduce-scatter.2.cloned.1.call-update) | async-done | bytes 32784 | tf_op jit(solution)/shard_map/reduce_scatter | solution.py:100
  464.8 0.8 add_convert_fusion
  465.6 0.6 reshape.161
  (14 shorter events, 0.1 us)
Async XLA Ops:
  7.2 237.0 %copy-start = (bf16[448,1024]{1,0:T(8,128)(2,1)S(1)}, bf16[448,1024]{1,0:T(8,128)(2,1)}, u32[]{:S(2)}) copy-start(bf16[448,1024]{1,0:T(8,128)(2,1)} %param.21) | copy-start | bytes 2752516
  11.1 20.4 %copy-start.10 = (s32[2,64]{1,0:T(2,128)S(1)}, s32[2,64]{1,0:T(2,128)}, u32[]{:S(2)}) copy-start(s32[2,64]{1,0:T(2,128)} %param.16) | copy-start | bytes 1540
  11.1 20.5 %copy-start.6 = (bf16[2,4,2,128]{3,2,1,0:T(2,128)(2,1)S(1)}, bf16[2,4,2,128]{3,2,1,0:T(2,128)(2,1)}, u32[]{:S(2)}) copy-start(bf16[2,4,2,128]{3,2,1,0:T(2,128)(2,1)} %param.12) | copy-start | bytes 12292
  11.1 20.5 %copy-start.4 = (bf16[2,4,1024]{2,1,0:T(4,128)(2,1)S(1)}, bf16[2,4,1024]{2,1,0:T(4,128)(2,1)}, u32[]{:S(2)}) copy-start(bf16[2,4,1024]{2,1,0:T(4,128)(2,1)} %param.11) | copy-start | bytes 49156
  11.1 20.5 %copy-start.1 = (bf16[64,2,16,128]{3,2,1,0:T(8,128)(2,1)S(1)}, bf16[64,2,16,128]{3,2,1,0:T(8,128)(2,1)}, u32[]{:S(2)}) copy-start(bf16[64,2,16,128]{3,2,1,0:T(8,128)(2,1)} %param.13) | copy-start | bytes 1572868
  12.6 20.7 %copy-start.11 = (s32[2]{0:T(128)S(1)}, s32[2]{0:T(128)}, u32[]{:S(2)}) copy-start(s32[2]{0:T(128)} %param.17) | copy-start | bytes 28
  12.6 75.0 %all-to-all-start = ((bf16[64,2,4096]{2,1,0:T(2,128)(2,1)}), bf16[64,2,4096]{2,1,0:T(2,128)(2,1)S(1)}, u32[]{:S(2)}, u32[]{:S(2)}) async-start(bf16[64,2,4096]{2,1,0:T(2,128)(2,1)} %reshape.150), calls=%async_computation | async-start | bytes 2097152 | tf_op jit(solution)/shard_map/all_to_all | solution.py:42
  31.6 3.7 copy-start.7
  90.6 0.7 copy-start.2
  90.6 1.0 copy-start.5
  90.6 1.0 copy-start.3
  90.9 1.3 copy-start.8
  91.9 7.0 %copy-start.9 = (bf16[1024]{0:T(1024)(128)(2,1)S(1)}, bf16[1024]{0:T(1024)(128)(2,1)}, u32[]{:S(2)}) copy-start(bf16[1024]{0:T(1024)(128)(2,1)} %param.18) | copy-start | bytes 6148
  91.9 63.1 %copy-start.12 = (bf16[1024,448]{0,1:T(8,128)(2,1)S(1)}, bf16[1024,448]{0,1:T(8,128)(2,1)}, u32[]{:S(2)}) copy-start(bf16[1024,448]{0,1:T(8,128)(2,1)} %param.20) | copy-start | bytes 2752516
  93.5 61.4 %all-to-all-start.1 = ((bf16[64,8,1024]{2,1,0:T(8,128)(2,1)}), bf16[64,8,1024]{2,1,0:T(8,128)(2,1)S(1)}, u32[]{:S(2)}, u32[]{:S(2)}) async-start(bf16[64,8,1024]{2,1,0:T(8,128)(2,1)} %stack.3), calls=%async_computation.1 | async-start | bytes 2097152 | tf_op jit(solution)/shard_map/all_to_all | solution.py:90
  98.8 145.4 %all-reduce.3.cloned.1.call-start = ((), (), s32[]{:S(2)}) async-start(), calls=%async_computation.4 | async-start | bytes 3670016 | tf_op jit(solution)/shard_map/psum | solution.py:97
  155.0 1.6 copy-start.13
  158.3 306.5 %reduce-scatter.2.cloned.1.call-start = ((), (), s32[]{:S(2)}) async-start(), calls=%async_computation.3 | async-start | bytes 2129920 | tf_op jit(solution)/shard_map/reduce_scatter | solution.py:100
Sparse Core Ops, SparseCore 0:
  158.4 85.7 all-reduce.2
  248.9 215.9 reduce-scatter.1
